TPU v7x, 32 devices: a whole 2x2x4 slice. The times are simulated.
32 devices in a mesh: node: 16 (over z, y, core), chip: 2 (over x).
Axes of the slice: x: 2, y: 2, z: 4, core: 2. Of those that a mesh axis runs over, the one named last changes fastest.
Arguments:
- tokens: bfloat16 [256, 3584], P(('node', 'chip')), may hold values from -6 to 6
- expert_ids: int32 [256, 8], P(('node', 'chip')), may hold values from 0 to 31, as said below
- gate_values: bfloat16 [256, 8], P(('node', 'chip')), may hold values from 0.099609375 to 1
- slot_ids: int32 [256, 8], P(('node', 'chip')), may hold values from 0 to 7, as said below
- up_weight: bfloat16 [32, 3584, 1024], P('node', None, 'chip'), may hold values from -0.09375 to 0.09375
- down_weight: bfloat16 [32, 1024, 3584], P('node', 'chip'), may hold values from -0.1875 to 0.1875
Outputs:
- mixed: bfloat16 [256, 3584], P(('node', 'chip'))
Inputs may be any that keep to these rules, and one draw needn't show every extreme that they name: `expert_ids`: each token's 8 entries name, in some order, all 2 experts of each of 4 distinct nodes. `slot_ids`: entries of one token that name experts of the same node hold the same slot; among the 16 tokens of one node (aligned blocks of the token dimension), the slots to one destination node are distinct, and some destination node receives all 8 slots from each source node.
All inputs are finite; a program needn't handle non-finite values.
Results may differ from a plain program's by a relative error of at most 0.0058.
Values may be sent and summed in bfloat16 or wider, within the bound.
A program may use at most 64 MiB of HBM per device.

v0:
```python
import jax
import jax.numpy as jnp
from jax import lax
from jax.sharding import PartitionSpec as P


def pack_rows(targets, experts, node_tokens, node_gates, row_count, per_node):
    row_ids = jnp.arange(row_count, dtype=jnp.int32)
    matches = (targets[None, :, :] == row_ids[:, None, None]).astype(jnp.bfloat16)
    picked = jnp.minimum(jnp.sum(matches.astype(jnp.float32), axis=2), 1.0).astype(jnp.bfloat16)
    packed = jnp.dot(picked, node_tokens, preferred_element_type=jnp.float32).astype(jnp.bfloat16)
    choose = (experts[:, :, None] == jnp.arange(per_node, dtype=jnp.int32)[None, None, :]).astype(
        jnp.bfloat16
    )
    weighted = choose * node_gates[:, :, None]
    gate_rows = jnp.einsum(
        "rtk,tke->re", matches, weighted, preferred_element_type=jnp.float32
    ).astype(jnp.bfloat16)
    return (packed, gate_rows)


def expert_rows(row_block, gate_block, up_local, down_local):
    result = jnp.zeros((row_block.shape[0], down_local.shape[2]), jnp.float32)
    for expert in range(up_local.shape[0]):
        hidden = jax.nn.silu(
            jnp.dot(row_block, up_local[expert], preferred_element_type=jnp.float32)
        ).astype(jnp.bfloat16)
        product = jnp.dot(hidden, down_local[expert], preferred_element_type=jnp.float32)
        result = result + gate_block[:, expert : expert + 1].astype(jnp.float32) * product
    return result.astype(jnp.bfloat16)


def gather_sum(indices, table):
    valid = indices >= 0
    safe = jnp.where(valid, indices, 0).reshape(-1)
    picked = jnp.take(table, safe, axis=0).reshape(
        indices.shape[0], indices.shape[1], table.shape[1]
    )
    return jnp.sum(jnp.where(valid[:, :, None], picked, 0.0), axis=1)


def shards(tokens, expert_ids, gate_values, slot_ids, up_weight, down_weight):
    node_count = lax.axis_size("node")
    chip_count = lax.axis_size("chip")
    my_chip = lax.axis_index("chip")
    tok_dev = tokens.shape[0]
    model_dim = tokens.shape[1]
    per_node = up_weight.shape[0]
    capacity = 8 * chip_count * tok_dev // node_count
    block_cap = capacity // chip_count
    route_code = (expert_ids // per_node * capacity + slot_ids) * per_node + expert_ids % per_node
    node_tokens, node_gates = (
        lax.all_gather(tokens, "chip", axis=0, tiled=True),
        lax.all_gather(gate_values, "chip", axis=0, tiled=True),
    )
    node_codes = lax.all_gather(route_code, "chip", axis=0, tiled=True)
    node_expert = node_codes % per_node
    node_slot = node_codes // per_node % capacity
    node_dest = node_codes // per_node // capacity
    targets = node_dest * capacity + node_slot
    packed, gate_rows = pack_rows(
        targets, node_expert, node_tokens, node_gates, node_count * capacity, per_node
    )
    shaped = packed.reshape(node_count, chip_count, 1, block_cap, model_dim)
    gate_shaped = gate_rows.reshape(node_count, chip_count, 1, block_cap, per_node)
    arrived, arrived_gates = (
        lax.all_to_all(shaped, "node", split_axis=0, concat_axis=2, tiled=True),
        lax.all_to_all(gate_shaped, "node", split_axis=0, concat_axis=2, tiled=True),
    )
    row_block = arrived.reshape(-1, model_dim)
    gate_block = arrived_gates.reshape(-1, per_node)
    partial_value = expert_rows(row_block, gate_block, up_weight, down_weight)
    pieces = lax.all_to_all(
        partial_value.reshape(chip_count, node_count * block_cap, model_dim),
        "chip",
        split_axis=0,
        concat_axis=0,
        tiled=True,
    )
    slot_sums = jnp.sum(pieces.astype(jnp.float32), axis=0).reshape(
        node_count, block_cap, model_dim
    )
    held = lax.all_to_all(slot_sums, "node", split_axis=0, concat_axis=0, tiled=True).reshape(
        node_count * block_cap, model_dim
    )
    wanted = (node_slot // block_cap == my_chip) & (node_expert == 0)
    indices = jnp.where(wanted, node_dest * block_cap + node_slot % block_cap, -1)
    term = gather_sum(indices, held)
    summed = lax.psum_scatter(term, "chip", scatter_dimension=0, tiled=True)
    return summed.astype(jnp.bfloat16)


def solution(mesh):
    return jax.shard_map(
        shards,
        mesh=mesh,
        in_specs=(
            P(("node", "chip"), None),
            P(("node", "chip"), None),
            P(("node", "chip"), None),
            P(("node", "chip"), None),
            P("node", None, "chip"),
            P("node", "chip", None),
        ),
        out_specs=P(("node", "chip"), None),
        check_vma=False,
    )
```

profile of v0, /device:TPU:0, one launch (start us, length us, event | category | flops | bytes accessed | tf_op | source)
XLA Modules:
  0.0 136.6 jit_solution(9596992641009980675)
XLA Ops:
  6.5 0.7 fusion.38
  7.3 5.3 %all_gather.9 = s32[16,8]{1,0:T(8,128)S(1)} all-gather(s32[8,8]{1,0:T(8,128)S(1)} %fusion.38), channel_id=1, replica_groups=mesh['node'=16,'chip'=2] {'chip'}, dimensions={0}, use_global_device_ids=true | all-gather | bytes 768 | tf_op jit(solution)/shard_map/all_gather | solution.py:56
  12.5 4.6 %all_gather.10 = bf16[16,8]{1,0:T(8,128)(2,1)S(1)} all-gather(bf16[8,8]{1,0:T(8,128)(2,1)} %param.8), channel_id=1, replica_groups=mesh['node'=16,'chip'=2] {'chip'}, dimensions={0}, use_global_device_ids=true | all-gather | bytes 384 | tf_op jit(solution)/shard_map/all_gather | solution.py:54
  17.1 0.1 copy.18
  17.2 0.1 copy.17
  17.3 0.1 copy.16
  17.4 0.2 fusion.14
  17.6 0.1 reshape.70
  17.7 0.6 copy.19
  18.3 6.4 %all-to-all-start = ((bf16[16,2,1,4,2]{3,1,4,2,0:T(2,128)(2,1)}), bf16[16,2,1,4,2]{3,1,4,2,0:T(2,128)(2,1)S(1)}, u32[]{:S(2)}, u32[]{:S(2)}) async-start(bf16[16,2,1,4,2]{3,1,4,2,0:T(2,128)(2,1)} %copy.19), calls=%async_computation | async-start | bytes 32768 | tf_op jit(solution)/shard_map/all_to_all | solution.py:68
  24.7 0.1 convert_reduce_fusion.1
  24.8 5.1 %all_gather.11 = bf16[16,3584]{1,0:T(8,128)(2,1)S(1)} all-gather(bf16[8,3584]{1,0:T(8,128)(2,1)} %param.6), channel_id=1, replica_groups=mesh['node'=16,'chip'=2] {'chip'}, dimensions={0}, use_global_device_ids=true | all-gather | bytes 172032 | tf_op jit(solution)/shard_map/all_gather | solution.py:53
  29.9 0.4 convolution_convert_fusion
  30.4 1.1 reshape.72
  31.5 0.0 all-to-all-done
  31.5 6.0 %all-to-all-start.1 = ((bf16[16,2,1,4,3584]{4,3,1,2,0:T(4,128)(2,1)}), bf16[16,2,1,4,3584]{4,3,1,2,0:T(4,128)(2,1)S(1)}, u32[]{:S(2)}, u32[]{:S(2)}) async-start(bf16[16,2,1,4,3584]{4,3,1,2,0:T(4,128)(2,1)} %bitcast.4), calls=%async_computation.1 | async-start | bytes 1835008 | tf_op jit(solution)/shard_map/all_to_all | solution.py:67
  37.5 0.1 reshape.71
  37.6 20.6 %all-to-all-done.1 = bf16[16,2,1,4,3584]{4,3,1,2,0:T(4,128)(2,1)S(1)} async-done(((bf16[16,2,1,4,3584]{4,3,1,2,0:T(4,128)(2,1)}), bf16[16,2,1,4,3584]{4,3,1,2,0:T(4,128)(2,1)S(1)}, u32[]{:S(2)}, u32[]{:S(2)}) %all-to-all-start.1) | async-done | bytes 917536 | tf_op jit(solution)/shard_map/all_to_all | solution.py:67
  58.3 0.3 copy.22
  58.6 0.2 reshape.73
  58.8 5.7 %convolution_multiply_fusion.1 = f32[128,3584]{1,0:T(8,128)} fusion(bf16[2,512,3584]{2,1,0:T(8,128)(2,1)} %param.11, f32[128]{0:T(128)S(1)} %get-tuple-element.10, bf16[128,3584]{1,0:T(8,128)(2,1)S(1)} %reshape.73, bf16[2,3584,512]{2,1,0:T(8,128)(2,1)} %param.10), kind=kOutput, calls=%fused_computation.3 | convolution fusion | flops 940310528 | bytes 10093056 | tf_op jit(solution)/shard_map/dot_general | solution.py:28
  64.5 4.9 %fusion.1 = bf16[128,3584]{1,0:T(8,128)(2,1)S(1)} fusion(f32[128,3584]{1,0:T(8,128)} %convolution_multiply_fusion.1, bf16[2,512,3584]{2,1,0:T(8,128)(2,1)} %param.11, f32[128]{0:T(128)S(1)} %get-tuple-element.9, bf16[128,3584]{1,0:T(8,128)(2,1)S(1)} %reshape.73, bf16[2,3584,512]{2,1,0:T(8,128)(2,1)} %param.10), kind=kOutput, calls=%fused_computation.4 | convolution fusion | flops 941228032 | bytes 11010560 | tf_op jit(solution)/shard_map/dot_general | solution.py:28
  69.5 15.6 %all_to_all.40 = bf16[2,64,3584]{2,1,0:T(8,128)(2,1)S(1)} all-to-all(bf16[2,64,3584]{2,1,0:T(8,128)(2,1)S(1)} %bitcast.58), channel_id=1, replica_groups=mesh['node'=16,'chip'=2] {'chip'}, dimensions={0} | all-to-all | bytes 1835008 | tf_op jit(solution)/shard_map/all_to_all | solution.py:73
  85.1 0.1 convert_reduce_fusion
  85.2 1.2 reshape.75
  86.4 5.9 %all-to-all-start.3 = ((f32[16,4,3584]{2,1,0:T(4,128)}), f32[16,4,3584]{2,1,0:T(4,128)S(1)}, u32[]{:S(2)}, u32[]{:S(2)}) async-start(f32[16,4,3584]{2,1,0:T(4,128)} %reshape.75), calls=%async_computation.3 | async-start | bytes 1835008 | tf_op jit(solution)/shard_map/all_to_all | solution.py:83
  92.4 0.0 reduce-scatter.2.cloned.1.call-start
  92.5 0.1 reshape.77
  92.6 20.5 %all-to-all-done.3 = f32[16,4,3584]{2,1,0:T(4,128)S(1)} async-done(((f32[16,4,3584]{2,1,0:T(4,128)}), f32[16,4,3584]{2,1,0:T(4,128)S(1)}, u32[]{:S(2)}, u32[]{:S(2)}) %all-to-all-start.3) | async-done | bytes 917536 | tf_op jit(solution)/shard_map/all_to_all | solution.py:83
  113.1 0.3 reshape.76
  113.5 1.3 gather_fusion
  114.7 1.4 %fusion.13 = f32[16,3584]{1,0:T(8,128)} fusion(f32[128,3584]{1,0:T(8,128)S(1)} %gather_fusion, pred[16,8]{1,0:T(8,128)(4,1)S(1)} %compare_and_fusion, pred[16,8]{1,0:T(8,128)(4,1)S(1)} %get-tuple-element.5), kind=kLoop, calls=%fused_computation.18 | loop fusion | flops 1318912 | bytes 2064640 | tf_op jit(solution)/shard_map/reduce_sum | solution.py:39
  116.2 0.0 reduce-scatter.2.cloned.1.call-update
  116.2 12.0 %reduce-scatter.2.cloned.1.call-done = f32[8,3584]{1,0:T(8,128)} async-done(((f32[16,3584]{1,0:T(8,128)}), f32[8,3584]{1,0:T(8,128)}) %reduce-scatter.2.cloned.1.call-update) | async-done | bytes 114704 | tf_op jit(solution)/shard_map/reduce_scatter | solution.py:89
  128.2 1.5 %convert_element_type.42 = bf16[8,3584]{1,0:T(8,128)(2,1)} convert(f32[8,3584]{1,0:T(8,128)} %reduce-scatter.2.cloned.1.call-done) | non-fusion elementwise | flops 28672 | bytes 172032 | tf_op jit(solution)/shard_map/convert_element_type | solution.py:90
  (8 shorter events, 0.1 us)
Async XLA Ops:
  18.3 13.2 %all-to-all-start = ((bf16[16,2,1,4,2]{3,1,4,2,0:T(2,128)(2,1)}), bf16[16,2,1,4,2]{3,1,4,2,0:T(2,128)(2,1)S(1)}, u32[]{:S(2)}, u32[]{:S(2)}) async-start(bf16[16,2,1,4,2]{3,1,4,2,0:T(2,128)(2,1)} %copy.19), calls=%async_computation | async-start | bytes 32768 | tf_op jit(solution)/shard_map/all_to_all | solution.py:68
  31.5 26.8 %all-to-all-start.1 = ((bf16[16,2,1,4,3584]{4,3,1,2,0:T(4,128)(2,1)}), bf16[16,2,1,4,3584]{4,3,1,2,0:T(4,128)(2,1)S(1)}, u32[]{:S(2)}, u32[]{:S(2)}) async-start(bf16[16,2,1,4,3584]{4,3,1,2,0:T(4,128)(2,1)} %bitcast.4), calls=%async_computation.1 | async-start | bytes 1835008 | tf_op jit(solution)/shard_map/all_to_all | solution.py:67
  86.4 26.7 %all-to-all-start.3 = ((f32[16,4,3584]{2,1,0:T(4,128)}), f32[16,4,3584]{2,1,0:T(4,128)S(1)}, u32[]{:S(2)}, u32[]{:S(2)}) async-start(f32[16,4,3584]{2,1,0:T(4,128)} %reshape.75), calls=%async_computation.3 | async-start | bytes 1835008 | tf_op jit(solution)/shard_map/all_to_all | solution.py:83
  92.4 35.9 %reduce-scatter.2.cloned.1.call-start = ((), (), s32[]{:S(2)}) async-start(), calls=%async_computation.5 | async-start | bytes 344064 | tf_op jit(solution)/shard_map/reduce_scatter | solution.py:89
Sparse Core Ops, SparseCore 0:
  116.3 11.8 reduce-scatter.1
where the time goes:
time: 137 us
  waiting for transfers between devices  53.3 us (39%)
  blocking collectives  30.6 us (22%)
  starting transfers between devices  18.4 us (13%)
  between operations  13.5 us (10%)
  matrix products  11.3 us (8%)
  local copies, waits for them, and re-layouts  5.6 us (4%)
  other arithmetic  3.99 us (3%)
    all_to_all x1, waiting for transfers between devices, shards(): lax.all_to_all(shaped, 'node', split_axis=0, concat_axis=2, tiled=True)  20.6 us
    all_to_all x1, waiting for transfers between devices, shards(): lax.all_to_all(slot_sums, 'node', split_axis=0, concat_axis=0, tiled=True)  20.5 us
    all_to_all x1, blocking collectives, shards(): lax.all_to_all(partial_value.reshape(chip_count, node_count * block_cap,...  15.6 us
    reduce_scatter x1, waiting for transfers between devices, shards(): summed = lax.psum_scatter(term, 'chip', scatter_dimension=0, tiled=True)  12 us
    dot_general x2, matrix products, expert_rows(): jnp.dot(hidden, down_local[expert], preferred_element_type=jnp.float32)  10.7 us
    all_to_all x1, starting transfers between devices, shards(): lax.all_to_all(gate_shaped, 'node', split_axis=0, concat_axis=2, tiled=True)  6.42 us
    all_to_all x1, starting transfers between devices, shards(): lax.all_to_all(shaped, 'node', split_axis=0, concat_axis=2, tiled=True)  5.97 us
    all_to_all x1, starting transfers between devices, shards(): lax.all_to_all(slot_sums, 'node', split_axis=0, concat_axis=0, tiled=True)  5.95 us
  transfers between devices with their start and end apart: 4, of which 3 were waited for; matrix products, arithmetic and copies ran while one was open for 1% of the time, Pallas kernels for 0%

commit v1 on v0

--- a/solution.py
+++ b/solution.py
@@ -1,7 +1,39 @@
+import functools
 import jax
 import jax.numpy as jnp
 from jax import lax
 from jax.sharding import PartitionSpec as P
+from jax.lax import axis_index, ppermute, psum
+
+
+def keep_up_the_sites(matrix, along_axis):
+    side_arr = psum(1, along_axis)
+    upper = axis_index(along_axis)
+    p_next, spare = (side_arr, upper)
+    t1 = list(matrix.shape)
+    b_now = matrix.shape[0] // p_next
+    t1[0] = b_now
+    z_new = t1[2]
+    t1[2] = z_new * p_next
+    dev_i = 0
+    right_arr = jnp.zeros(t1, matrix.dtype)
+    while dev_i < p_next:
+        kept_arr = lax.dynamic_slice_in_dim(matrix, (spare ^ dev_i) * b_now, b_now, axis=0)
+        if dev_i:
+            xs_all = []
+            t = 0
+            while t < p_next:
+                xs_all.append((t, t ^ dev_i))
+                t += 1
+            kept_arr = ppermute(kept_arr, along_axis, xs_all)
+        right_arr = lax.dynamic_update_slice_in_dim(
+            right_arr, kept_arr, (spare ^ dev_i) * z_new, axis=2
+        )
+        dev_i += 1
+    return right_arr
+
+
+rest_shelves = functools.partial(keep_up_the_sites, along_axis="node")
 
 
 def pack_rows(targets, experts, node_tokens, node_gates, row_count, per_node):
@@ -64,7 +96,7 @@
     shaped = packed.reshape(node_count, chip_count, 1, block_cap, model_dim)
     gate_shaped = gate_rows.reshape(node_count, chip_count, 1, block_cap, per_node)
     arrived, arrived_gates = (
-        lax.all_to_all(shaped, "node", split_axis=0, concat_axis=2, tiled=True),
+        rest_shelves(shaped),
         lax.all_to_all(gate_shaped, "node", split_axis=0, concat_axis=2, tiled=True),
     )
     row_block = arrived.reshape(-1, model_dim)

time: 137 us -> 167 us (1.22)
  waiting for transfers between devices: 53.3 us -> 72.6 us
  starting transfers between devices: 18.4 us -> 28.9 us
    ppermute x0 -> x15, waiting for transfers between devices: none -> 40 us  [keep_up_the_sites(): kept_arr = ppermute(kept_arr, along_axis, xs_all)]
    all_to_all x1 -> x0, waiting for transfers between devices: 20.6 us -> none  [shards(): lax.all_to_all(shaped, 'node', split_axis=0, concat_axis=2, tiled=True)]
    ppermute x0 -> x15, starting transfers between devices: none -> 18.8 us  [keep_up_the_sites(): kept_arr = ppermute(kept_arr, along_axis, xs_all)]
    all_to_all x1 -> x0, starting transfers between devices: 5.97 us -> none  [shards(): lax.all_to_all(shaped, 'node', split_axis=0, concat_axis=2, tiled=True)]
    all_to_all x1, starting transfers between devices: 5.95 us -> 3.63 us  [shards(): lax.all_to_all(slot_sums, 'node', split_axis=0, concat_axis=0, tiled=True)]
  transfers between devices with their start and end apart: 4 -> 18, of which waited for: 3 -> 13; matrix products, arithmetic and copies ran while one was open for 1% -> 1% of each run, Pallas kernels for 0% -> 0%
where the time goes in v1:
time: 167 us; the launch traced here: 166 us
  waiting for transfers between devices  72.6 us (43%)
  blocking collectives  30.1 us (18%)
  starting transfers between devices  28.9 us (17%)
  between operations  13.7 us (8%)
  matrix products  11.3 us (7%)
  local copies, waits for them, and re-layouts  5.51 us (3%)
  other arithmetic  4.01 us (2%)
    ppermute x15, waiting for transfers between devices, keep_up_the_sites(): kept_arr = ppermute(kept_arr, along_axis, xs_all)  40 us
    all_to_all x1, waiting for transfers between devices, shards(): lax.all_to_all(slot_sums, 'node', split_axis=0, concat_axis=0, tiled=True)  20.6 us
    ppermute x15, starting transfers between devices, keep_up_the_sites(): kept_arr = ppermute(kept_arr, along_axis, xs_all)  18.8 us
    all_to_all x1, blocking collectives, shards(): lax.all_to_all(partial_value.reshape(chip_count, node_count * block_cap,...  15.2 us
    reduce_scatter x1, waiting for transfers between devices, shards(): summed = lax.psum_scatter(term, 'chip', scatter_dimension=0, tiled=True)  12 us
    dot_general x2, matrix products, expert_rows(): jnp.dot(hidden, down_local[expert], preferred_element_type=jnp.float32)  10.7 us
    all_to_all x1, starting transfers between devices, shards(): lax.all_to_all(gate_shaped, 'node', split_axis=0, concat_axis=2, tiled=True)  6.42 us
    all_gather x1, blocking collectives, shards(): node_codes = lax.all_gather(route_code, 'chip', axis=0, tiled=True)  5.28 us
  transfers between devices with their start and end apart: 18, of which 13 were waited for; matrix products, arithmetic and copies ran while one was open for 1% of the time, Pallas kernels for 0%

profile of v1, /device:TPU:0, one launch (start us, length us, event | category | flops | bytes accessed | tf_op | source)
XLA Modules:
  0.0 166.1 jit_solution(4830878216480357934)
XLA Ops:
  6.5 0.7 fusion.38
  7.3 5.3 %all_gather.9 = s32[16,8]{1,0:T(8,128)S(1)} all-gather(s32[8,8]{1,0:T(8,128)S(1)} %fusion.38), channel_id=1, replica_groups=mesh['node'=16,'chip'=2] {'chip'}, dimensions={0}, use_global_device_ids=true | all-gather | bytes 768 | tf_op jit(solution)/shard_map/all_gather | solution.py:88
  12.5 4.6 %all_gather.10 = bf16[16,8]{1,0:T(8,128)(2,1)S(1)} all-gather(bf16[8,8]{1,0:T(8,128)(2,1)} %param.8), channel_id=1, replica_groups=mesh['node'=16,'chip'=2] {'chip'}, dimensions={0}, use_global_device_ids=true | all-gather | bytes 384 | tf_op jit(solution)/shard_map/all_gather | solution.py:86
  17.4 0.2 fusion.14
  17.6 0.1 reshape.69
  17.7 0.6 copy.34
  18.3 6.4 %all-to-all-start = ((bf16[16,2,1,4,2]{3,1,4,2,0:T(2,128)(2,1)}), bf16[16,2,1,4,2]{3,1,4,2,0:T(2,128)(2,1)S(1)}, u32[]{:S(2)}, u32[]{:S(2)}) async-start(bf16[16,2,1,4,2]{3,1,4,2,0:T(2,128)(2,1)} %copy.34), calls=%async_computation | async-start | bytes 32768 | tf_op jit(solution)/shard_map/all_to_all | solution.py:100
  24.9 5.1 %all_gather.11 = bf16[16,3584]{1,0:T(8,128)(2,1)S(1)} all-gather(bf16[8,3584]{1,0:T(8,128)(2,1)} %param.6), channel_id=1, replica_groups=mesh['node'=16,'chip'=2] {'chip'}, dimensions={0}, use_global_device_ids=true | all-gather | bytes 172032 | tf_op jit(solution)/shard_map/all_gather | solution.py:85
  30.0 0.4 convolution_convert_fusion
  30.4 0.2 reshape.71
  30.7 0.2 broadcast_in_dim.36
  31.0 0.4 constant_dynamic-slice_fusion
  31.4 3.2 %collective-permute-start.14 = (bf16[1,2,1,4,3584]{4,3,2,1,0:T(4,128)(2,1)S(1)}, bf16[1,2,1,4,3584]{4,3,2,1,0:T(4,128)(2,1)S(1)}, u32[]{:S(2)}, u32[]{:S(2)}) collective-permute-start(bf16[1,2,1,4,3584]{4,3,2,1,0:T(4,128)(2,1)S(1)} %get-tuple-element.7), channel_id=1, source_target_pairs={{0,30},{2,28},{4,26},{6,24},{8,22},{10,20},{12,18},{14,16},{16,14}... | collective-permute-start | bytes 172040 | tf_op jit(solution)/shard_map/ppermute | solution.py:28
  34.6 1.5 collective-permute-start.13
  36.1 3.2 %collective-permute-start.12 = (bf16[1,2,1,4,3584]{4,3,2,1,0:T(4,128)(2,1)S(1)}, bf16[1,2,1,4,3584]{4,3,2,1,0:T(4,128)(2,1)S(1)}, u32[]{:S(2)}, u32[]{:S(2)}) collective-permute-start(bf16[1,2,1,4,3584]{4,3,2,1,0:T(4,128)(2,1)S(1)} %get-tuple-element.9), channel_id=1, source_target_pairs={{0,26},{2,24},{4,30},{6,28},{8,18},{10,16},{12,22},{14,20},{16,10}... | collective-permute-start | bytes 172040 | tf_op jit(solution)/shard_map/ppermute | solution.py:28
  39.3 0.3 collective-permute-start.11
  39.5 0.2 collective-permute-start
  39.9 0.9 collective-permute-done
  40.8 1.7 %collective-permute-start.1 = (bf16[1,2,1,4,3584]{4,3,2,1,0:T(4,128)(2,1)S(1)}, bf16[1,2,1,4,3584]{4,3,2,1,0:T(4,128)(2,1)S(1)}, u32[]{:S(2)}, u32[]{:S(2)}) collective-permute-start(bf16[1,2,1,4,3584]{4,3,2,1,0:T(4,128)(2,1)S(1)} %get-tuple-element.20), channel_id=1, source_target_pairs={{0,4},{2,6},{4,0},{6,2},{8,12},{10,14},{12,8},{14,10},{16,20},{18,... | collective-permute-start | bytes 172040 | tf_op jit(solution)/shard_map/ppermute | solution.py:28
  42.6 2.4 %collective-permute-done.1 = bf16[1,2,1,4,3584]{4,3,2,1,0:T(4,128)(2,1)S(1)} collective-permute-done((bf16[1,2,1,4,3584]{4,3,2,1,0:T(4,128)(2,1)S(1)}, bf16[1,2,1,4,3584]{4,3,2,1,0:T(4,128)(2,1)S(1)}, u32[]{:S(2)}, u32[]{:S(2)}) %collective-permute-start.1) | collective-permute-done | bytes 57376 | tf_op jit(solution)/shard_map/ppermute | solution.py:28
  45.0 0.6 collective-permute-start.2
  45.6 3.3 %collective-permute-done.2 = bf16[1,2,1,4,3584]{4,3,2,1,0:T(4,128)(2,1)S(1)} collective-permute-done((bf16[1,2,1,4,3584]{4,3,2,1,0:T(4,128)(2,1)S(1)}, bf16[1,2,1,4,3584]{4,3,2,1,0:T(4,128)(2,1)S(1)}, u32[]{:S(2)}, u32[]{:S(2)}) %collective-permute-start.2) | collective-permute-done | bytes 57376 | tf_op jit(solution)/shard_map/ppermute | solution.py:28
  48.9 4.1 %collective-permute-done.3 = bf16[1,2,1,4,3584]{4,3,2,1,0:T(4,128)(2,1)S(1)} collective-permute-done((bf16[1,2,1,4,3584]{4,3,2,1,0:T(4,128)(2,1)S(1)}, bf16[1,2,1,4,3584]{4,3,2,1,0:T(4,128)(2,1)S(1)}, u32[]{:S(2)}, u32[]{:S(2)}) %collective-permute-start.3) | collective-permute-done | bytes 57376 | tf_op jit(solution)/shard_map/ppermute | solution.py:28
  53.1 3.6 %collective-permute-done.4 = bf16[1,2,1,4,3584]{4,3,2,1,0:T(4,128)(2,1)S(1)} collective-permute-done((bf16[1,2,1,4,3584]{4,3,2,1,0:T(4,128)(2,1)S(1)}, bf16[1,2,1,4,3584]{4,3,2,1,0:T(4,128)(2,1)S(1)}, u32[]{:S(2)}, u32[]{:S(2)}) %collective-permute-start.4) | collective-permute-done | bytes 57376 | tf_op jit(solution)/shard_map/ppermute | solution.py:28
  56.7 1.0 collective-permute-start.5
  57.7 4.1 %collective-permute-done.5 = bf16[1,2,1,4,3584]{4,3,2,1,0:T(4,128)(2,1)S(1)} collective-permute-done((bf16[1,2,1,4,3584]{4,3,2,1,0:T(4,128)(2,1)S(1)}, bf16[1,2,1,4,3584]{4,3,2,1,0:T(4,128)(2,1)S(1)}, u32[]{:S(2)}, u32[]{:S(2)}) %collective-permute-start.5) | collective-permute-done | bytes 57376 | tf_op jit(solution)/shard_map/ppermute | solution.py:28
  61.8 0.2 collective-permute-start.6
  62.0 4.3 %collective-permute-done.6 = bf16[1,2,1,4,3584]{4,3,2,1,0:T(4,128)(2,1)S(1)} collective-permute-done((bf16[1,2,1,4,3584]{4,3,2,1,0:T(4,128)(2,1)S(1)}, bf16[1,2,1,4,3584]{4,3,2,1,0:T(4,128)(2,1)S(1)}, u32[]{:S(2)}, u32[]{:S(2)}) %collective-permute-start.6) | collective-permute-done | bytes 57376 | tf_op jit(solution)/shard_map/ppermute | solution.py:28
  66.3 2.9 %collective-permute-start.7 = (bf16[1,2,1,4,3584]{4,3,2,1,0:T(4,128)(2,1)S(1)}, bf16[1,2,1,4,3584]{4,3,2,1,0:T(4,128)(2,1)S(1)}, u32[]{:S(2)}, u32[]{:S(2)}) collective-permute-start(bf16[1,2,1,4,3584]{4,3,2,1,0:T(4,128)(2,1)S(1)} %get-tuple-element.14), channel_id=1, source_target_pairs={{0,16},{2,18},{4,20},{6,22},{8,24},{10,26},{12,28},{14,30},{16,0},... | collective-permute-start | bytes 172040 | tf_op jit(solution)/shard_map/ppermute | solution.py:28
  69.2 2.4 %collective-permute-done.7 = bf16[1,2,1,4,3584]{4,3,2,1,0:T(4,128)(2,1)S(1)} collective-permute-done((bf16[1,2,1,4,3584]{4,3,2,1,0:T(4,128)(2,1)S(1)}, bf16[1,2,1,4,3584]{4,3,2,1,0:T(4,128)(2,1)S(1)}, u32[]{:S(2)}, u32[]{:S(2)}) %collective-permute-start.7) | collective-permute-done | bytes 57376 | tf_op jit(solution)/shard_map/ppermute | solution.py:28
  71.6 1.1 collective-permute-start.8
  72.8 3.5 %collective-permute-done.8 = bf16[1,2,1,4,3584]{4,3,2,1,0:T(4,128)(2,1)S(1)} collective-permute-done((bf16[1,2,1,4,3584]{4,3,2,1,0:T(4,128)(2,1)S(1)}, bf16[1,2,1,4,3584]{4,3,2,1,0:T(4,128)(2,1)S(1)}, u32[]{:S(2)}, u32[]{:S(2)}) %collective-permute-start.8) | collective-permute-done | bytes 57376 | tf_op jit(solution)/shard_map/ppermute | solution.py:28
  76.3 2.8 %collective-permute-start.9 = (bf16[1,2,1,4,3584]{4,3,2,1,0:T(4,128)(2,1)S(1)}, bf16[1,2,1,4,3584]{4,3,2,1,0:T(4,128)(2,1)S(1)}, u32[]{:S(2)}, u32[]{:S(2)}) collective-permute-start(bf16[1,2,1,4,3584]{4,3,2,1,0:T(4,128)(2,1)S(1)} %get-tuple-element.12), channel_id=1, source_target_pairs={{0,20},{2,22},{4,16},{6,18},{8,28},{10,30},{12,24},{14,26},{16,4},... | collective-permute-start | bytes 172040 | tf_op jit(solution)/shard_map/ppermute | solution.py:28
  79.1 4.5 %collective-permute-done.9 = bf16[1,2,1,4,3584]{4,3,2,1,0:T(4,128)(2,1)S(1)} collective-permute-done((bf16[1,2,1,4,3584]{4,3,2,1,0:T(4,128)(2,1)S(1)}, bf16[1,2,1,4,3584]{4,3,2,1,0:T(4,128)(2,1)S(1)}, u32[]{:S(2)}, u32[]{:S(2)}) %collective-permute-start.9) | collective-permute-done | bytes 57376 | tf_op jit(solution)/shard_map/ppermute | solution.py:28
  83.6 7.0 %collective-permute-done.10 = bf16[1,2,1,4,3584]{4,3,2,1,0:T(4,128)(2,1)S(1)} collective-permute-done((bf16[1,2,1,4,3584]{4,3,2,1,0:T(4,128)(2,1)S(1)}, bf16[1,2,1,4,3584]{4,3,2,1,0:T(4,128)(2,1)S(1)}, u32[]{:S(2)}, u32[]{:S(2)}) %collective-permute-start.10) | collective-permute-done | bytes 57376 | tf_op jit(solution)/shard_map/ppermute | solution.py:28
  90.9 0.2 reshape.72
  91.1 5.7 %convolution_multiply_fusion.1 = f32[128,3584]{1,0:T(8,128)} fusion(bf16[2,512,3584]{2,1,0:T(8,128)(2,1)} %param.11, f32[128]{0:T(128)S(1)} %get-tuple-element.26, bf16[128,3584]{1,0:T(8,128)(2,1)S(1)} %reshape.72, bf16[2,3584,512]{2,1,0:T(8,128)(2,1)} %param.10), kind=kOutput, calls=%fused_computation.3 | convolution fusion | flops 940310528 | bytes 10093056 | tf_op jit(solution)/shard_map/dot_general | solution.py:60
  96.8 4.9 %fusion.1 = bf16[128,3584]{1,0:T(8,128)(2,1)S(1)} fusion(f32[128,3584]{1,0:T(8,128)} %convolution_multiply_fusion.1, bf16[2,512,3584]{2,1,0:T(8,128)(2,1)} %param.11, f32[128]{0:T(128)S(1)} %get-tuple-element.25, bf16[128,3584]{1,0:T(8,128)(2,1)S(1)} %reshape.72, bf16[2,3584,512]{2,1,0:T(8,128)(2,1)} %param.10), kind=kOutput, calls=%fused_computation.4 | convolution fusion | flops 941228032 | bytes 11010560 | tf_op jit(solution)/shard_map/dot_general | solution.py:60
  101.8 15.2 %all_to_all.25 = bf16[2,64,3584]{2,1,0:T(8,128)(2,1)S(1)} all-to-all(bf16[2,64,3584]{2,1,0:T(8,128)(2,1)S(1)} %bitcast.68), channel_id=1, replica_groups=mesh['node'=16,'chip'=2] {'chip'}, dimensions={0} | all-to-all | bytes 1835008 | tf_op jit(solution)/shard_map/all_to_all | solution.py:105
  117.0 0.1 convert_reduce_fusion
  117.1 1.2 reshape.74
  118.3 3.6 %all-to-all-start.2 = ((f32[16,4,3584]{2,1,0:T(4,128)}), f32[16,4,3584]{2,1,0:T(4,128)S(1)}, u32[]{:S(2)}, u32[]{:S(2)}) async-start(f32[16,4,3584]{2,1,0:T(4,128)} %reshape.74), calls=%async_computation.2 | async-start | bytes 1835008 | tf_op jit(solution)/shard_map/all_to_all | solution.py:115
  122.1 20.6 %all-to-all-done.2 = f32[16,4,3584]{2,1,0:T(4,128)S(1)} async-done(((f32[16,4,3584]{2,1,0:T(4,128)}), f32[16,4,3584]{2,1,0:T(4,128)S(1)}, u32[]{:S(2)}, u32[]{:S(2)}) %all-to-all-start.2) | async-done | bytes 917536 | tf_op jit(solution)/shard_map/all_to_all | solution.py:115
  142.7 0.3 reshape.75
  143.0 1.3 gather_fusion
  144.3 1.5 fusion.13
  145.8 12.0 %reduce-scatter.2.cloned.1.call-done = f32[8,3584]{1,0:T(8,128)} async-done(((f32[16,3584]{1,0:T(8,128)}), f32[8,3584]{1,0:T(8,128)}) %reduce-scatter.2.cloned.1.call-update) | async-done | bytes 114704 | tf_op jit(solution)/shard_map/reduce_scatter | solution.py:121
  157.8 1.5 convert_element_type.42
  (38 shorter events, 1.2 us)
Async XLA Ops:
  18.3 21.4 %all-to-all-start = ((bf16[16,2,1,4,2]{3,1,4,2,0:T(2,128)(2,1)}), bf16[16,2,1,4,2]{3,1,4,2,0:T(2,128)(2,1)S(1)}, u32[]{:S(2)}, u32[]{:S(2)}) async-start(bf16[16,2,1,4,2]{3,1,4,2,0:T(2,128)(2,1)} %copy.34), calls=%async_computation | async-start | bytes 32768 | tf_op jit(solution)/shard_map/all_to_all | solution.py:100
  31.4 59.4 %collective-permute-start.14 = (bf16[1,2,1,4,3584]{4,3,2,1,0:T(4,128)(2,1)S(1)}, bf16[1,2,1,4,3584]{4,3,2,1,0:T(4,128)(2,1)S(1)}, u32[]{:S(2)}, u32[]{:S(2)}) collective-permute-start(bf16[1,2,1,4,3584]{4,3,2,1,0:T(4,128)(2,1)S(1)} %get-tuple-element.7), channel_id=1, source_target_pairs={{0,30},{2,28},{4,26},{6,24},{8,22},{10,20},{12,18},{14,16},{16,14}... | collective-permute-start | bytes 172040 | tf_op jit(solution)/shard_map/ppermute | solution.py:28
  34.6 56.2 %collective-permute-start.13 = (bf16[1,2,1,4,3584]{4,3,2,1,0:T(4,128)(2,1)S(1)}, bf16[1,2,1,4,3584]{4,3,2,1,0:T(4,128)(2,1)S(1)}, u32[]{:S(2)}, u32[]{:S(2)}) collective-permute-start(bf16[1,2,1,4,3584]{4,3,2,1,0:T(4,128)(2,1)S(1)} %get-tuple-element.8), channel_id=1, source_target_pairs={{0,28},{2,30},{4,24},{6,26},{8,20},{10,22},{12,16},{14,18},{16,12}... | collective-permute-start | bytes 172040 | tf_op jit(solution)/shard_map/ppermute | solution.py:28
  36.1 54.6 %collective-permute-start.12 = (bf16[1,2,1,4,3584]{4,3,2,1,0:T(4,128)(2,1)S(1)}, bf16[1,2,1,4,3584]{4,3,2,1,0:T(4,128)(2,1)S(1)}, u32[]{:S(2)}, u32[]{:S(2)}) collective-permute-start(bf16[1,2,1,4,3584]{4,3,2,1,0:T(4,128)(2,1)S(1)} %get-tuple-element.9), channel_id=1, source_target_pairs={{0,26},{2,24},{4,30},{6,28},{8,18},{10,16},{12,22},{14,20},{16,10}... | collective-permute-start | bytes 172040 | tf_op jit(solution)/shard_map/ppermute | solution.py:28
  39.3 51.4 %collective-permute-start.11 = (bf16[1,2,1,4,3584]{4,3,2,1,0:T(4,128)(2,1)S(1)}, bf16[1,2,1,4,3584]{4,3,2,1,0:T(4,128)(2,1)S(1)}, u32[]{:S(2)}, u32[]{:S(2)}) collective-permute-start(bf16[1,2,1,4,3584]{4,3,2,1,0:T(4,128)(2,1)S(1)} %get-tuple-element.10), channel_id=1, source_target_pairs={{0,24},{2,26},{4,28},{6,30},{8,16},{10,18},{12,20},{14,22},{16,8},... | collective-permute-start | bytes 172040 | tf_op jit(solution)/shard_map/ppermute | solution.py:28
  39.5 1.2 collective-permute-start
  40.8 4.2 %collective-permute-start.1 = (bf16[1,2,1,4,3584]{4,3,2,1,0:T(4,128)(2,1)S(1)}, bf16[1,2,1,4,3584]{4,3,2,1,0:T(4,128)(2,1)S(1)}, u32[]{:S(2)}, u32[]{:S(2)}) collective-permute-start(bf16[1,2,1,4,3584]{4,3,2,1,0:T(4,128)(2,1)S(1)} %get-tuple-element.20), channel_id=1, source_target_pairs={{0,4},{2,6},{4,0},{6,2},{8,12},{10,14},{12,8},{14,10},{16,20},{18,... | collective-permute-start | bytes 172040 | tf_op jit(solution)/shard_map/ppermute | solution.py:28
  45.0 3.9 %collective-permute-start.2 = (bf16[1,2,1,4,3584]{4,3,2,1,0:T(4,128)(2,1)S(1)}, bf16[1,2,1,4,3584]{4,3,2,1,0:T(4,128)(2,1)S(1)}, u32[]{:S(2)}, u32[]{:S(2)}) collective-permute-start(bf16[1,2,1,4,3584]{4,3,2,1,0:T(4,128)(2,1)S(1)} %get-tuple-element.19), channel_id=1, source_target_pairs={{0,6},{2,4},{4,2},{6,0},{8,14},{10,12},{12,10},{14,8},{16,22},{18,... | collective-permute-start | bytes 172040 | tf_op jit(solution)/shard_map/ppermute | solution.py:28
  48.9 4.2 %collective-permute-start.3 = (bf16[1,2,1,4,3584]{4,3,2,1,0:T(4,128)(2,1)S(1)}, bf16[1,2,1,4,3584]{4,3,2,1,0:T(4,128)(2,1)S(1)}, u32[]{:S(2)}, u32[]{:S(2)}) collective-permute-start(bf16[1,2,1,4,3584]{4,3,2,1,0:T(4,128)(2,1)S(1)} %get-tuple-element.18), channel_id=1, source_target_pairs={{0,8},{2,10},{4,12},{6,14},{8,0},{10,2},{12,4},{14,6},{16,24},{18,... | collective-permute-start | bytes 172040 | tf_op jit(solution)/shard_map/ppermute | solution.py:28
  53.1 3.6 %collective-permute-start.4 = (bf16[1,2,1,4,3584]{4,3,2,1,0:T(4,128)(2,1)S(1)}, bf16[1,2,1,4,3584]{4,3,2,1,0:T(4,128)(2,1)S(1)}, u32[]{:S(2)}, u32[]{:S(2)}) collective-permute-start(bf16[1,2,1,4,3584]{4,3,2,1,0:T(4,128)(2,1)S(1)} %get-tuple-element.17), channel_id=1, source_target_pairs={{0,10},{2,8},{4,14},{6,12},{8,2},{10,0},{12,6},{14,4},{16,26},{18,... | collective-permute-start | bytes 172040 | tf_op jit(solution)/shard_map/ppermute | solution.py:28
  56.7 5.1 %collective-permute-start.5 = (bf16[1,2,1,4,3584]{4,3,2,1,0:T(4,128)(2,1)S(1)}, bf16[1,2,1,4,3584]{4,3,2,1,0:T(4,128)(2,1)S(1)}, u32[]{:S(2)}, u32[]{:S(2)}) collective-permute-start(bf16[1,2,1,4,3584]{4,3,2,1,0:T(4,128)(2,1)S(1)} %get-tuple-element.16), channel_id=1, source_target_pairs={{0,12},{2,14},{4,8},{6,10},{8,4},{10,6},{12,0},{14,2},{16,28},{18,... | collective-permute-start | bytes 172040 | tf_op jit(solution)/shard_map/ppermute | solution.py:28
  61.8 4.5 %collective-permute-start.6 = (bf16[1,2,1,4,3584]{4,3,2,1,0:T(4,128)(2,1)S(1)}, bf16[1,2,1,4,3584]{4,3,2,1,0:T(4,128)(2,1)S(1)}, u32[]{:S(2)}, u32[]{:S(2)}) collective-permute-start(bf16[1,2,1,4,3584]{4,3,2,1,0:T(4,128)(2,1)S(1)} %get-tuple-element.15), channel_id=1, source_target_pairs={{0,14},{2,12},{4,10},{6,8},{8,6},{10,4},{12,2},{14,0},{16,30},{18,... | collective-permute-start | bytes 172040 | tf_op jit(solution)/shard_map/ppermute | solution.py:28
  66.3 5.3 %collective-permute-start.7 = (bf16[1,2,1,4,3584]{4,3,2,1,0:T(4,128)(2,1)S(1)}, bf16[1,2,1,4,3584]{4,3,2,1,0:T(4,128)(2,1)S(1)}, u32[]{:S(2)}, u32[]{:S(2)}) collective-permute-start(bf16[1,2,1,4,3584]{4,3,2,1,0:T(4,128)(2,1)S(1)} %get-tuple-element.14), channel_id=1, source_target_pairs={{0,16},{2,18},{4,20},{6,22},{8,24},{10,26},{12,28},{14,30},{16,0},... | collective-permute-start | bytes 172040 | tf_op jit(solution)/shard_map/ppermute | solution.py:28
  71.6 4.7 %collective-permute-start.8 = (bf16[1,2,1,4,3584]{4,3,2,1,0:T(4,128)(2,1)S(1)}, bf16[1,2,1,4,3584]{4,3,2,1,0:T(4,128)(2,1)S(1)}, u32[]{:S(2)}, u32[]{:S(2)}) collective-permute-start(bf16[1,2,1,4,3584]{4,3,2,1,0:T(4,128)(2,1)S(1)} %get-tuple-element.13), channel_id=1, source_target_pairs={{0,18},{2,16},{4,22},{6,20},{8,26},{10,24},{12,30},{14,28},{16,2},... | collective-permute-start | bytes 172040 | tf_op jit(solution)/shard_map/ppermute | solution.py:28
  76.3 7.3 %collective-permute-start.9 = (bf16[1,2,1,4,3584]{4,3,2,1,0:T(4,128)(2,1)S(1)}, bf16[1,2,1,4,3584]{4,3,2,1,0:T(4,128)(2,1)S(1)}, u32[]{:S(2)}, u32[]{:S(2)}) collective-permute-start(bf16[1,2,1,4,3584]{4,3,2,1,0:T(4,128)(2,1)S(1)} %get-tuple-element.12), channel_id=1, source_target_pairs={{0,20},{2,22},{4,16},{6,18},{8,28},{10,30},{12,24},{14,26},{16,4},... | collective-permute-start | bytes 172040 | tf_op jit(solution)/shard_map/ppermute | solution.py:28
  83.6 7.1 %collective-permute-start.10 = (bf16[1,2,1,4,3584]{4,3,2,1,0:T(4,128)(2,1)S(1)}, bf16[1,2,1,4,3584]{4,3,2,1,0:T(4,128)(2,1)S(1)}, u32[]{:S(2)}, u32[]{:S(2)}) collective-permute-start(bf16[1,2,1,4,3584]{4,3,2,1,0:T(4,128)(2,1)S(1)} %get-tuple-element.11), channel_id=1, source_target_pairs={{0,22},{2,20},{4,18},{6,16},{8,30},{10,28},{12,26},{14,24},{16,6},... | collective-permute-start | bytes 172040 | tf_op jit(solution)/shard_map/ppermute | solution.py:28
  118.3 24.4 %all-to-all-start.2 = ((f32[16,4,3584]{2,1,0:T(4,128)}), f32[16,4,3584]{2,1,0:T(4,128)S(1)}, u32[]{:S(2)}, u32[]{:S(2)}) async-start(f32[16,4,3584]{2,1,0:T(4,128)} %reshape.74), calls=%async_computation.2 | async-start | bytes 1835008 | tf_op jit(solution)/shard_map/all_to_all | solution.py:115
  121.9 35.8 %reduce-scatter.2.cloned.1.call-start = ((), (), s32[]{:S(2)}) async-start(), calls=%async_computation.4 | async-start | bytes 344064 | tf_op jit(solution)/shard_map/reduce_scatter | solution.py:121
Sparse Core Ops, SparseCore 0:
  145.9 11.8 reduce-scatter.1
